TPU v7x, 32 devices: a whole 2x2x4 slice. The times are simulated.
32 devices in a mesh: region: 2 (over y), tile: 4 (over z), member: 2 (over x), date: 2 (over core).
Axes of the slice: x: 2, y: 2, z: 4, core: 2. Of those that a mesh axis runs over, the one named last changes fastest.
Arguments:
- sim_lai: bfloat16 [2, 32, 4, 32, 512], P('date', ('region', 'tile'), 'member'), parts along dimension 1, may hold values from 0 to 6
- owner_ids: int32 [2, 32], P('date', ('region', 'tile')), parts along dimension 1, may hold values from 0 to 3, as said below
- cloud_words: int32 [2, 32, 32], P('date', ('region', 'tile')), parts along dimension 1, may hold values from -2147483648 to 2147483646
- scene_lai: bfloat16 [2, 8, 8, 16, 256], P('date', ('region', 'tile'), 'member'), parts along dimension 1, may hold values from 0 to 6
- scene_sigma: bfloat16 [2, 8, 8, 16, 256], P('date', ('region', 'tile'), 'member'), parts along dimension 1, may hold values from 1 to 4
- mtf_taps: float32 [2, 7], replicated, may hold values from 0.1 to 1
Outputs:
- lai_update: bfloat16 [2, 32, 4, 32, 512], P('date', ('region', 'tile'), 'member'), parts along dimension 1
There are 2 independent parts, one for each index of `region`. A program takes and returns all parts, laid end to end along the dimension named above; an argument that names none is the same for every part. Nothing has to cross between parts.
Inputs may be any that keep to these rules, and one draw needn't show every extreme that they name: `owner_ids`: on each date each device along tile, holding 4 consecutive tiles, sends either none or exactly 2 of them to each owner; some owner receives 2 tiles from every device.
All inputs are finite; a program needn't handle non-finite values.
Results may differ from a plain program's by a relative error of at most 0.013.
The roundings to bfloat16 on the way count: a program that leaves them out, or rounds other values in their place, can miss the bound.
Values may be sent and summed in bfloat16 or wider, within the bound.
No kernel may reach another device: no remote copies, remote signals or barrier semaphores. Data moves between devices by JAX's collectives and lax.ppermute only.
A program may use at most 64 MiB of HBM per device.

v0:
```python
import jax
import jax.numpy as jnp
from jax import lax
from jax.sharding import PartitionSpec as P

CAP = 2


def band_tables(mtf_taps, tile_rows, tile_cols):
    kernel = mtf_taps / jnp.sum(mtf_taps, axis=1, keepdims=True)
    half_rows = tile_rows // 2
    half_cols = tile_cols // 2
    tap_reach = mtf_taps.shape[1] // 2
    out_rows = lax.broadcasted_iota(jnp.int32, (half_rows, tile_rows), 0)
    in_rows = lax.broadcasted_iota(jnp.int32, (half_rows, tile_rows), 1)
    in_cols = lax.broadcasted_iota(jnp.int32, (tile_cols, half_cols), 0)
    out_cols = lax.broadcasted_iota(jnp.int32, (tile_cols, half_cols), 1)
    row_table = jnp.zeros((half_rows, tile_rows), jnp.float32)
    col_table = jnp.zeros((tile_cols, half_cols), jnp.float32)
    for offset in range(mtf_taps.shape[1]):
        row_table = row_table + jnp.where(
            in_rows == 2 * out_rows + offset - tap_reach, kernel[0, offset], 0.0
        )
        col_table = col_table + jnp.where(
            in_cols == 2 * out_cols + offset - tap_reach, kernel[1, offset], 0.0
        )
    return (row_table.astype(jnp.bfloat16), col_table.astype(jnp.bfloat16))


def cloud_weights(words, half_rows, half_cols):
    shifts = jnp.arange(32)
    bit_values = jnp.bitwise_and(jnp.right_shift(words[..., None], shifts), 1)
    cells = bit_values.reshape(words.shape[:-1] + (half_rows // 2, half_cols // 2)).astype(
        jnp.float32
    )
    return jnp.repeat(jnp.repeat(cells, 2, axis=-2), 2, axis=-1)


def weighted_misfit(valid, observed, sigma_obs, predicted):
    sigma_wide = sigma_obs.astype(jnp.float32)
    gap = observed.astype(jnp.float32) - predicted.astype(jnp.float32)
    return (valid * gap / (sigma_wide * sigma_wide)).astype(jnp.bfloat16)


def degrade(fields, row_table, col_table):
    blurred = jnp.einsum(
        "ir,...rc->...ic", row_table, fields, preferred_element_type=jnp.float32
    ).astype(jnp.bfloat16)
    return jnp.einsum(
        "...ic,cj->...ij", blurred, col_table, preferred_element_type=jnp.float32
    ).astype(jnp.bfloat16)


def adjoint_map(misfit, row_table, col_table):
    spread = jnp.einsum(
        "...ij,cj->...ic", misfit, col_table, preferred_element_type=jnp.float32
    ).astype(jnp.bfloat16)
    return jnp.einsum(
        "ir,...ic->...rc", row_table, spread, preferred_element_type=jnp.float32
    ).astype(jnp.bfloat16)


def per_device(sim_lai, owner_ids, cloud_words, scene_lai, scene_sigma, mtf_taps):
    tile_count = lax.axis_size("tile")
    tiles_here = sim_lai.shape[1]
    members_here = sim_lai.shape[2]
    tile_rows = sim_lai.shape[3]
    tile_cols = sim_lai.shape[4]
    half_rows = tile_rows // 2
    half_cols = tile_cols // 2
    slot_count = tile_count * CAP
    row_table, col_table = band_tables(mtf_taps, tile_rows, tile_cols)
    owners = owner_ids[0]
    same_owner = owners[:, None] == owners[None, :]
    earlier = lax.broadcasted_iota(jnp.int32, (tiles_here, tiles_here), 0) < lax.broadcasted_iota(
        jnp.int32, (tiles_here, tiles_here), 1
    )
    rank = jnp.sum(jnp.logical_and(same_owner, earlier).astype(jnp.int32), axis=0)
    target = owners * CAP + rank
    slot_onehot = lax.broadcasted_iota(jnp.int32, (slot_count, tiles_here), 0) == target[None, :]
    onehot_bf = slot_onehot.astype(jnp.bfloat16)
    scenes, sigmas = (
        lax.all_gather(scene_lai, "member", axis=2, tiled=True),
        lax.all_gather(scene_sigma, "member", axis=2, tiled=True),
    )
    local_tiles = sim_lai[0]
    words_out = jnp.sum(jnp.where(slot_onehot[:, :, None], cloud_words[0][None, :, :], 0), axis=1)
    words_out = words_out.reshape(tile_count, CAP, -1)
    scenes = scenes.reshape(slot_count, 1, half_rows, half_cols)
    sigmas = sigmas.reshape(slot_count, 1, half_rows, half_cols)
    flat = local_tiles.reshape(tiles_here, -1)
    outgoing = (
        jnp.dot(onehot_bf, flat, preferred_element_type=jnp.float32)
        .astype(jnp.bfloat16)
        .reshape(tile_count, CAP, members_here, tile_rows, tile_cols)
    )
    arrived, arrived_words = (
        lax.all_to_all(outgoing, "tile", split_axis=0, concat_axis=0, tiled=True),
        lax.all_to_all(words_out, "tile", split_axis=0, concat_axis=0, tiled=True),
    )
    arrived = arrived.reshape(slot_count, members_here, tile_rows, tile_cols)
    valid = cloud_weights(arrived_words.reshape(slot_count, -1), half_rows, half_cols)[:, None]
    misfit = weighted_misfit(valid, scenes, sigmas, degrade(arrived, row_table, col_table))
    answered = adjoint_map(misfit, row_table, col_table).reshape(
        tile_count, CAP, members_here, tile_rows, tile_cols
    )
    returned = lax.all_to_all(answered, "tile", split_axis=0, concat_axis=0, tiled=True)
    flat = returned.reshape(slot_count, -1)
    lai_update = (
        jnp.dot(onehot_bf.T, flat, preferred_element_type=jnp.float32)
        .astype(jnp.bfloat16)
        .reshape(tiles_here, members_here, tile_rows, tile_cols)
    )
    return lai_update[None]


def solution(mesh):
    placed = (
        P("date", ("region", "tile"), "member", None, None),
        P("date", ("region", "tile")),
        P("date", ("region", "tile"), None),
        P("date", ("region", "tile"), "member", None, None),
        P("date", ("region", "tile"), "member", None, None),
        P(),
    )
    return jax.shard_map(
        per_device,
        mesh=mesh,
        in_specs=placed,
        out_specs=P("date", ("region", "tile"), "member", None, None),
        check_vma=False,
    )
```

profile of v0, /device:TPU:0, one launch (start us, length us, event | category | flops | bytes accessed | tf_op | source)
XLA Modules:
  0.0 74.5 jit_solution(14291288457161708068)
XLA Ops:
  0.0 0.0 copy-start.4
  0.0 0.7 copy-done.4
  0.7 0.1 convert_reduce_fusion
  0.7 0.0 copy-start.3
  0.8 0.1 iota_compare_fusion.15
  0.8 0.6 copy-done.3
  1.4 0.7 select_reduce_fusion
  2.1 6.3 %all-to-all-start = ((s32[4,2,32]{2,1,0:T(2,128)}), s32[4,2,32]{2,1,0:T(2,128)S(1)}, u32[]{:S(2)}, u32[]{:S(2)}) async-start(s32[4,2,32]{2,1,0:T(2,128)} %bitcast.4), calls=%async_computation | async-start | bytes 8192 | tf_op jit(solution)/shard_map/all_to_all | solution.py:99
  8.5 0.0 copy-start.2
  8.5 0.7 copy-done.2
  9.2 0.1 reduce_sum.32
  9.3 0.1 broadcast_divide_fusion
  9.3 0.7 fusion.27
  10.0 1.1 %reshape_squeeze.3 = bf16[4,32768]{1,0:T(4,128)(2,1)S(1)} reshape(bf16[1,4,2,32,512]{4,3,2,1,0:T(8,128)(2,1)} %param.6) | data formatting | bytes 524288 | tf_op jit(solution)/shard_map/reshape;squeeze | solution.py:91
  11.2 0.0 copy-start
  11.2 0.4 convolution_convert_fusion
  11.6 0.3 copy-done
  11.9 0.0 copy-start.1
  11.9 4.7 %all_gather.6 = bf16[1,1,8,16,256]{4,3,1,0,2:T(8,128)(2,1)S(1)} all-gather(bf16[1,1,4,16,256]{4,3,1,0,2:T(8,128)(2,1)S(1)} %bitcast.87), channel_id=1, replica_groups=mesh['region'=2,'tile'=4,'member'=2,'date'=2] {'member'}, dimensions={2}, use_global_device_ids=true | all-gather | bytes 98304 | tf_op jit(solution)/shard_map/all_gather | solution.py:83
  16.7 0.0 copy-done.1
  16.7 4.6 %all_gather.7 = bf16[1,1,8,16,256]{4,3,1,0,2:T(8,128)(2,1)S(1)} all-gather(bf16[1,1,4,16,256]{4,3,1,0,2:T(8,128)(2,1)S(1)} %bitcast.88), channel_id=1, replica_groups=mesh['region'=2,'tile'=4,'member'=2,'date'=2] {'member'}, dimensions={2}, use_global_device_ids=true | all-gather | bytes 98304 | tf_op jit(solution)/shard_map/all_gather | solution.py:84
  21.2 0.1 shift_right_arithmetic.26
  21.3 0.9 %copy.23 = bf16[1,8,64,512]{3,2,1,0:T(8,128)(2,1)} copy(bf16[1,8,64,512]{3,1,2,0:T(8,128)(2,1)S(1)} %bitcast.82) | data formatting | bytes 1048576
  22.3 0.0 all-to-all-done
  22.3 5.1 %all-to-all-start.1 = ((bf16[4,2,2,32,512]{4,3,2,1,0:T(8,128)(2,1)}), bf16[4,2,2,32,512]{4,3,2,1,0:T(8,128)(2,1)S(1)}, u32[]{:S(2)}, u32[]{:S(2)}) async-start(bf16[4,2,2,32,512]{4,3,2,1,0:T(8,128)(2,1)} %bitcast.41), calls=%async_computation.1 | async-start | bytes 1048576 | tf_op jit(solution)/shard_map/all_to_all | solution.py:98
  27.4 0.1 shift_right_arithmetic.23
  27.5 0.1 shift_right_arithmetic.24
  27.6 0.2 copy.17
  27.9 0.1 broadcast_in_dim.101
  28.0 0.4 copy.18
  28.3 10.7 %all-to-all-done.1 = bf16[4,2,2,32,512]{4,3,2,1,0:T(8,128)(2,1)S(1)} async-done(((bf16[4,2,2,32,512]{4,3,2,1,0:T(8,128)(2,1)}), bf16[4,2,2,32,512]{4,3,2,1,0:T(8,128)(2,1)S(1)}, u32[]{:S(2)}, u32[]{:S(2)}) %all-to-all-start.1) | async-done | bytes 524320 | tf_op jit(solution)/shard_map/all_to_all | solution.py:98
  39.0 9.3 %fusion.7 = bf16[8,2,16,256]{3,2,1,0:T(8,128)(2,1)S(1)} fusion(bf16[8,2,32,512]{3,2,1,0:T(8,128)(2,1)S(1)} %bitcast.84, f32[]{:T(128)} %bitcast.27, s32[256]{0:T(256)S(1)} %get-tuple-element.20, f32[]{:T(128)} %bitcast.26, s32[256]{0:T(256)S(1)} %get-tuple-element.21, f32[]{:T(128)} %bitcast.25, s32[256]{0:T(256)S(1)} %get-tuple-element.22, f32[]{:T(128)} %bitcast.24, ...), kind=kOutput, calls=%fused_computation.12 | convolution fusion | flops 78785024 | bytes 1056248 | tf_op jit(solution)/shard_map/...ic,cj->...ij/dot_general | solution.py:49
  48.3 9.3 %convolution_convert_fusion.2 = bf16[8,2,512,32]{2,3,1,0:T(8,128)(2,1)S(1)} fusion(bf16[8,2,16,256]{3,2,1,0:T(8,128)(2,1)S(1)} %fusion.7, f32[]{:T(128)} %bitcast.27, s32[256]{0:T(256)S(1)} %get-tuple-element.20, f32[]{:T(128)} %bitcast.26, s32[256]{0:T(256)S(1)} %get-tuple-element.21, f32[]{:T(128)} %bitcast.25, s32[256]{0:T(256)S(1)} %get-tuple-element.22, ...), kind=kOutput, calls=%fused_computation.2 | convolution fusion | flops 78653952 | bytes 663032 | tf_op jit(solution)/shard_map/ir,...ic->...rc/dot_general | solution.py:58
  57.6 15.5 %all_to_all.15 = bf16[4,2,2,32,512]{4,3,2,1,0:T(8,128)(2,1)S(1)} all-to-all(bf16[4,2,2,32,512]{4,3,2,1,0:T(8,128)(2,1)S(1)} %bitcast.85), channel_id=1, replica_groups=mesh['region'=2,'tile'=4,'member'=2,'date'=2] {'tile'}, dimensions={0} | all-to-all | bytes 1048576 | tf_op jit(solution)/shard_map/all_to_all | solution.py:107
  73.1 0.2 reshape.71
  73.4 0.4 convolution_convert_fusion.1
  73.7 0.7 %copy.24 = bf16[1,4,64,512]{3,2,1,0:T(8,128)(2,1)} copy(bf16[1,4,64,512]{3,1,2,0:T(4,128)(2,1)S(1)} %bitcast.83) | data formatting | bytes 524288
  (15 shorter events, 0.1 us)
Async XLA Ops:
  0.0 0.7 copy-start.4
  0.7 0.7 copy-start.3
  2.1 20.2 %all-to-all-start = ((s32[4,2,32]{2,1,0:T(2,128)}), s32[4,2,32]{2,1,0:T(2,128)S(1)}, u32[]{:S(2)}, u32[]{:S(2)}) async-start(s32[4,2,32]{2,1,0:T(2,128)} %bitcast.4), calls=%async_computation | async-start | bytes 8192 | tf_op jit(solution)/shard_map/all_to_all | solution.py:99
  8.5 0.7 copy-start.2
  11.2 0.8 %copy-start = (bf16[1,1,4,16,256]{4,3,2,1,0:T(8,128)(2,1)S(1)}, bf16[1,1,4,16,256]{4,3,2,1,0:T(8,128)(2,1)}, u32[]{:S(2)}) copy-start(bf16[1,1,4,16,256]{4,3,2,1,0:T(8,128)(2,1)} %param.9) | copy-start | bytes 98308
  11.9 4.7 %copy-start.1 = (bf16[1,1,4,16,256]{4,3,2,1,0:T(8,128)(2,1)S(1)}, bf16[1,1,4,16,256]{4,3,2,1,0:T(8,128)(2,1)}, u32[]{:S(2)}) copy-start(bf16[1,1,4,16,256]{4,3,2,1,0:T(8,128)(2,1)} %param.10) | copy-start | bytes 98308
  22.3 16.7 %all-to-all-start.1 = ((bf16[4,2,2,32,512]{4,3,2,1,0:T(8,128)(2,1)}), bf16[4,2,2,32,512]{4,3,2,1,0:T(8,128)(2,1)S(1)}, u32[]{:S(2)}, u32[]{:S(2)}) async-start(bf16[4,2,2,32,512]{4,3,2,1,0:T(8,128)(2,1)} %bitcast.41), calls=%async_computation.1 | async-start | bytes 1048576 | tf_op jit(solution)/shard_map/all_to_all | solution.py:98
where the time goes:
time: 75.2 us; the launch traced here: 74.5 us
  blocking collectives  24.8 us (33%)
  matrix products  19.4 us (26%)
  starting transfers between devices  11.4 us (15%)
  waiting for transfers between devices  10.7 us (14%)
  local copies, waits for them, and re-layouts  6.98 us (9%)
  other arithmetic  1.09 us (1%)
    all_to_all x1, blocking collectives, per_device(): lax.all_to_all(answered, 'tile', split_axis=0, concat_axis=0, tiled=True)  15.5 us
    all_to_all x1, waiting for transfers between devices, per_device(): lax.all_to_all(outgoing, 'tile', split_axis=0, concat_axis=0, tiled=True)  10.7 us
    dot_general x1, matrix products, degrade(): jnp.einsum('...ic,cj->...ij', blurred, col_table, preferred_element_type=...  9.32 us
    dot_general x1, matrix products, adjoint_map(): jnp.einsum('ir,...ic->...rc', row_table, spread, preferred_element_type=j...  9.32 us
    all_to_all x1, starting transfers between devices, per_device(): lax.all_to_all(words_out, 'tile', split_axis=0, concat_axis=0, tiled=True)  6.32 us
    all_to_all x1, starting transfers between devices, per_device(): lax.all_to_all(outgoing, 'tile', split_axis=0, concat_axis=0, tiled=True)  5.08 us
    all_gather x1, blocking collectives, per_device(): lax.all_gather(scene_lai, 'member', axis=2, tiled=True)  4.71 us
    all_gather x1, blocking collectives, per_device(): lax.all_gather(scene_sigma, 'member', axis=2, tiled=True)  4.58 us
  transfers between devices with their start and end apart: 2, of which 1 were waited for; matrix products, arithmetic and copies ran while one was open for 6% of the time, Pallas kernels for 0%

commit v1 on v0

--- a/solution.py
+++ b/solution.py
@@ -4,6 +4,18 @@
 from jax.sharding import PartitionSpec as P
 
 CAP = 2
+
+
+def gather_by_bits(x, axis, dim):
+    ways, here = (lax.axis_size(axis), lax.axis_index(axis))
+    grown, reach = (x, 1)
+    while reach < ways:
+        theirs = lax.ppermute(grown, axis, [(d, d ^ reach) for d in range(ways)])
+        mine_first = jnp.concatenate([grown, theirs], axis=dim)
+        theirs_first = jnp.concatenate([theirs, grown], axis=dim)
+        grown = jnp.where(here & reach == 0, mine_first, theirs_first)
+        reach = 2 * reach
+    return grown
 
 
 def band_tables(mtf_taps, tile_rows, tile_cols):
@@ -80,7 +92,7 @@
     slot_onehot = lax.broadcasted_iota(jnp.int32, (slot_count, tiles_here), 0) == target[None, :]
     onehot_bf = slot_onehot.astype(jnp.bfloat16)
     scenes, sigmas = (
-        lax.all_gather(scene_lai, "member", axis=2, tiled=True),
+        gather_by_bits(scene_lai, "member", 2),
         lax.all_gather(scene_sigma, "member", axis=2, tiled=True),
     )
     local_tiles = sim_lai[0]

time: 75.2 us -> 72.3 us (0.961)
  blocking collectives: 24.8 us -> 20.1 us
  starting transfers between devices: 11.4 us -> 12.9 us
    all_gather x1 -> x0, blocking collectives: 4.71 us -> none  [per_device(): lax.all_gather(scene_lai, 'member', axis=2, tiled=True)]
    ppermute x0 -> x1, starting transfers between devices: none -> 1.49 us  [gather_by_bits(): theirs = lax.ppermute(grown, axis, [(d, d ^ reach) for d in range(ways)])]
  transfers between devices with their start and end apart: 2 -> 3, of which waited for: 1 -> 1; matrix products, arithmetic and copies ran while one was open for 6% -> 6% of each run, Pallas kernels for 0% -> 0%
where the time goes in v1:
time: 72.3 us; the launch traced here: 71.5 us
  blocking collectives  20.1 us (28%)
  matrix products  19.5 us (27%)
  starting transfers between devices  12.9 us (18%)
  waiting for transfers between devices  10.4 us (14%)
  local copies, waits for them, and re-layouts  7.39 us (10%)
  other arithmetic  1.09 us (2%)
    all_to_all x1, blocking collectives, per_device(): lax.all_to_all(answered, 'tile', split_axis=0, concat_axis=0, tiled=True)  15.5 us
    all_to_all x1, waiting for transfers between devices, per_device(): lax.all_to_all(outgoing, 'tile', split_axis=0, concat_axis=0, tiled=True)  10.4 us
    dot_general x1, matrix products, degrade(): jnp.einsum('...ic,cj->...ij', blurred, col_table, preferred_element_type=...  9.35 us
    dot_general x1, matrix products, adjoint_map(): jnp.einsum('ir,...ic->...rc', row_table, spread, preferred_element_type=j...  9.35 us
    all_to_all x1, starting transfers between devices, per_device(): lax.all_to_all(words_out, 'tile', split_axis=0, concat_axis=0, tiled=True)  6.32 us
    all_to_all x1, starting transfers between devices, per_device(): lax.all_to_all(outgoing, 'tile', split_axis=0, concat_axis=0, tiled=True)  5.09 us
    all_gather x1, blocking collectives, per_device(): lax.all_gather(scene_sigma, 'member', axis=2, tiled=True)  4.58 us
    unnamed x12, local copies, waits for them, and re-layouts  4.37 us
  transfers between devices with their start and end apart: 3, of which 1 were waited for; matrix products, arithmetic and copies ran while one was open for 6% of the time, Pallas kernels for 0%

profile of v1, /device:TPU:0, one launch (start us, length us, event | category | flops | bytes accessed | tf_op | source)
XLA Modules:
  0.0 71.5 jit_solution(306743701810885015)
XLA Ops:
  0.0 0.0 copy-start.4
  0.0 0.7 copy-done.4
  0.7 0.1 convert_reduce_fusion
  0.7 0.0 copy-start.3
  0.8 0.1 iota_compare_fusion.15
  0.8 0.6 copy-done.3
  1.4 0.7 select_reduce_fusion
  2.1 6.3 %all-to-all-start = ((s32[4,2,32]{2,1,0:T(2,128)}), s32[4,2,32]{2,1,0:T(2,128)S(1)}, u32[]{:S(2)}, u32[]{:S(2)}) async-start(s32[4,2,32]{2,1,0:T(2,128)} %bitcast.4), calls=%async_computation | async-start | bytes 8192 | tf_op jit(solution)/shard_map/all_to_all | solution.py:111
  8.4 1.5 %collective-permute-start = (bf16[1,1,4,16,256]{4,3,2,1,0:T(8,128)(2,1)}, bf16[1,1,4,16,256]{4,3,2,1,0:T(8,128)(2,1)S(1)}, u32[]{:S(2)}, u32[]{:S(2)}) collective-permute-start(bf16[1,1,4,16,256]{4,3,2,1,0:T(8,128)(2,1)} %param.9), channel_id=1, source_target_pairs={{0,2},{2,0},{1,3},{3,1},{4,6},{6,4},{5,7},{7,5},{8,10},{10,8},{9,1... | collective-permute-start | bytes 98312 | tf_op jit(solution)/shard_map/ppermute | solution.py:13
  10.0 0.0 copy-start.2
  10.0 0.7 copy-done.2
  10.6 0.1 reduce_sum.32
  10.8 0.1 broadcast_divide_fusion
  10.8 1.1 %reshape_squeeze.3 = bf16[4,32768]{1,0:T(4,128)(2,1)S(1)} reshape(bf16[1,4,2,32,512]{4,3,2,1,0:T(8,128)(2,1)} %param.6) | data formatting | bytes 524288 | tf_op jit(solution)/shard_map/reshape;squeeze | solution.py:103
  12.0 0.0 copy-start
  12.0 0.4 convolution_convert_fusion
  12.4 0.3 copy-done
  12.7 4.6 %all_gather.3 = bf16[1,1,8,16,256]{4,3,1,0,2:T(8,128)(2,1)S(1)} all-gather(bf16[1,1,4,16,256]{4,3,1,0,2:T(8,128)(2,1)S(1)} %bitcast.85), channel_id=1, replica_groups=mesh['region'=2,'tile'=4,'member'=2,'date'=2] {'member'}, dimensions={2}, use_global_device_ids=true | all-gather | bytes 98304 | tf_op jit(solution)/shard_map/all_gather | solution.py:96
  17.3 0.1 shift_right_arithmetic.26
  17.4 1.0 %copy.21 = bf16[1,8,64,512]{3,2,1,0:T(8,128)(2,1)} copy(bf16[1,8,64,512]{3,1,2,0:T(8,128)(2,1)S(1)} %bitcast.80) | data formatting | bytes 1048576
  18.4 0.0 all-to-all-done
  18.4 5.1 %all-to-all-start.1 = ((bf16[4,2,2,32,512]{4,3,2,1,0:T(8,128)(2,1)}), bf16[4,2,2,32,512]{4,3,2,1,0:T(8,128)(2,1)S(1)}, u32[]{:S(2)}, u32[]{:S(2)}) async-start(bf16[4,2,2,32,512]{4,3,2,1,0:T(8,128)(2,1)} %bitcast.40), calls=%async_computation.1 | async-start | bytes 1048576 | tf_op jit(solution)/shard_map/all_to_all | solution.py:110
  23.5 0.7 fusion.28
  24.2 0.1 shift_right_arithmetic.23
  24.3 0.1 shift_right_arithmetic.24
  24.4 0.2 copy.16
  24.7 0.1 broadcast_in_dim.101
  24.7 0.0 copy-start.1
  24.8 0.4 copy.17
  25.1 0.0 collective-permute-done
  25.1 0.4 copy-done.1
  25.5 10.4 %all-to-all-done.1 = bf16[4,2,2,32,512]{4,3,2,1,0:T(8,128)(2,1)S(1)} async-done(((bf16[4,2,2,32,512]{4,3,2,1,0:T(8,128)(2,1)}), bf16[4,2,2,32,512]{4,3,2,1,0:T(8,128)(2,1)S(1)}, u32[]{:S(2)}, u32[]{:S(2)}) %all-to-all-start.1) | async-done | bytes 524320 | tf_op jit(solution)/shard_map/all_to_all | solution.py:110
  36.0 9.4 %fusion.7 = bf16[8,2,16,256]{3,2,1,0:T(8,128)(2,1)S(1)} fusion(bf16[8,2,32,512]{3,2,1,0:T(8,128)(2,1)S(1)} %bitcast.82, f32[]{:T(128)} %bitcast.27, s32[256]{0:T(256)S(1)} %get-tuple-element.19, f32[]{:T(128)} %bitcast.26, s32[256]{0:T(256)S(1)} %get-tuple-element.20, f32[]{:T(128)} %bitcast.25, s32[256]{0:T(256)S(1)} %get-tuple-element.21, f32[]{:T(128)} %bitcast.24, ...), kind=kOutput, calls=%fused_computation.12 | convolution fusion | flops 78785024 | bytes 1056248 | tf_op jit(solution)/shard_map/...ic,cj->...ij/dot_general | solution.py:61
  45.3 9.3 %convolution_convert_fusion.2 = bf16[8,2,512,32]{2,3,1,0:T(8,128)(2,1)S(1)} fusion(bf16[8,2,16,256]{3,2,1,0:T(8,128)(2,1)S(1)} %fusion.7, f32[]{:T(128)} %bitcast.27, s32[256]{0:T(256)S(1)} %get-tuple-element.19, f32[]{:T(128)} %bitcast.26, s32[256]{0:T(256)S(1)} %get-tuple-element.20, f32[]{:T(128)} %bitcast.25, s32[256]{0:T(256)S(1)} %get-tuple-element.21, ...), kind=kOutput, calls=%fused_computation.2 | convolution fusion | flops 78653952 | bytes 663032 | tf_op jit(solution)/shard_map/ir,...ic->...rc/dot_general | solution.py:70
  54.7 15.5 %all_to_all.15 = bf16[4,2,2,32,512]{4,3,2,1,0:T(8,128)(2,1)S(1)} all-to-all(bf16[4,2,2,32,512]{4,3,2,1,0:T(8,128)(2,1)S(1)} %bitcast.83), channel_id=1, replica_groups=mesh['region'=2,'tile'=4,'member'=2,'date'=2] {'tile'}, dimensions={0} | all-to-all | bytes 1048576 | tf_op jit(solution)/shard_map/all_to_all | solution.py:119
  70.2 0.2 reshape.119
  70.4 0.3 convolution_convert_fusion.1
  70.8 0.7 %copy.22 = bf16[1,4,64,512]{3,2,1,0:T(8,128)(2,1)} copy(bf16[1,4,64,512]{3,1,2,0:T(4,128)(2,1)S(1)} %bitcast.81) | data formatting | bytes 524288
  (15 shorter events, 0.1 us)
Async XLA Ops:
  0.0 0.7 copy-start.4
  0.7 0.7 copy-start.3
  2.1 16.3 %all-to-all-start = ((s32[4,2,32]{2,1,0:T(2,128)}), s32[4,2,32]{2,1,0:T(2,128)S(1)}, u32[]{:S(2)}, u32[]{:S(2)}) async-start(s32[4,2,32]{2,1,0:T(2,128)} %bitcast.4), calls=%async_computation | async-start | bytes 8192 | tf_op jit(solution)/shard_map/all_to_all | solution.py:111
  8.4 16.7 %collective-permute-start = (bf16[1,1,4,16,256]{4,3,2,1,0:T(8,128)(2,1)}, bf16[1,1,4,16,256]{4,3,2,1,0:T(8,128)(2,1)S(1)}, u32[]{:S(2)}, u32[]{:S(2)}) collective-permute-start(bf16[1,1,4,16,256]{4,3,2,1,0:T(8,128)(2,1)} %param.9), channel_id=1, source_target_pairs={{0,2},{2,0},{1,3},{3,1},{4,6},{6,4},{5,7},{7,5},{8,10},{10,8},{9,1... | collective-permute-start | bytes 98312 | tf_op jit(solution)/shard_map/ppermute | solution.py:13
  10.0 0.7 copy-start.2
  12.0 0.8 %copy-start = (bf16[1,1,4,16,256]{4,3,2,1,0:T(8,128)(2,1)S(1)}, bf16[1,1,4,16,256]{4,3,2,1,0:T(8,128)(2,1)}, u32[]{:S(2)}) copy-start(bf16[1,1,4,16,256]{4,3,2,1,0:T(8,128)(2,1)} %param.10) | copy-start | bytes 98308
  18.4 17.6 %all-to-all-start.1 = ((bf16[4,2,2,32,512]{4,3,2,1,0:T(8,128)(2,1)}), bf16[4,2,2,32,512]{4,3,2,1,0:T(8,128)(2,1)S(1)}, u32[]{:S(2)}, u32[]{:S(2)}) async-start(bf16[4,2,2,32,512]{4,3,2,1,0:T(8,128)(2,1)} %bitcast.40), calls=%async_computation.1 | async-start | bytes 1048576 | tf_op jit(solution)/shard_map/all_to_all | solution.py:110
  24.7 0.8 %copy-start.1 = (bf16[1,1,4,16,256]{4,3,2,1,0:T(8,128)(2,1)S(1)}, bf16[1,1,4,16,256]{4,3,2,1,0:T(8,128)(2,1)}, u32[]{:S(2)}) copy-start(bf16[1,1,4,16,256]{4,3,2,1,0:T(8,128)(2,1)} %param.9) | copy-start | bytes 98308
